TPU v7x, 512 devices: a whole 4x8x8 slice. The times are simulated.
512 devices in a mesh: blk: 32 (over x, y_lo, core), fsdp: 16 (over z, y_hi).
Axes of the slice: x: 4, y: 8 (y_hi: 2, y_lo: 4; y = y_hi * 4 + y_lo), z: 8, core: 2. Of those that a mesh axis runs over, the one named last changes fastest.
Arguments:
- decoder_states: bfloat16 [8192, 4096], P('blk', 'fsdp'), may hold values from -10 to 10
- w_query: bfloat16 [4096, 4096], P('blk', 'fsdp'), may hold values from -0.09375 to 0.09375
- w_out_t: bfloat16 [4096, 4096], P('blk', 'fsdp'), may hold values from -0.1875 to 0.1875
- enc_keys: bfloat16 [8192, 4096], P('blk', 'fsdp'), may hold values from -80 to 80
- enc_values: bfloat16 [8192, 4096], P('blk', 'fsdp'), may hold values from -6 to 6
Outputs:
- attended: bfloat16 [8192, 4096], P(('blk', 'fsdp'))
All inputs are finite; a program needn't handle non-finite values.
Results may differ from a plain program's by a relative error of at most 0.0095.
Values may be sent and summed in bfloat16 or wider, within the bound.
A program may use at most 128 MiB of HBM per device.

v0:
```python
import math

import jax
import jax.numpy as jnp
from jax import lax
from jax.sharding import PartitionSpec as P

HEAD_DIM = 64


def absorb(fold_state, query_heads, key_rows, value_rows):
    running_top, running_sum, weighted = fold_state
    local_heads = query_heads.shape[1]
    key_heads = key_rows.reshape(key_rows.shape[0], local_heads, HEAD_DIM)
    value_heads = value_rows.reshape(value_rows.shape[0], local_heads, HEAD_DIM)
    scores = jnp.einsum(
        "qhd,khd->hqk", query_heads, key_heads, preferred_element_type=jnp.float32
    ) * (1.0 / math.sqrt(HEAD_DIM))
    new_top = jnp.max(scores, axis=2)
    rescale = jnp.exp(running_top - new_top)
    probability = jnp.exp(scores - new_top[:, :, None])
    running_sum = running_sum * rescale + jnp.sum(probability, axis=2)
    weighted = weighted * rescale[:, :, None] + jnp.einsum(
        "hqk,khd->hqd",
        probability.astype(jnp.bfloat16),
        value_heads,
        preferred_element_type=jnp.float32,
    )
    return (new_top, running_sum, weighted)


def shards(decoder_states, w_query, w_out_t, enc_keys, enc_values):
    query_full = lax.all_gather(w_query, "blk", axis=0, tiled=True)
    row_count = decoder_states.shape[0]
    columns = query_full.shape[1]
    local_heads = columns // HEAD_DIM
    queries = jnp.dot(
        lax.all_gather(decoder_states, "fsdp", axis=1, tiled=True),
        query_full,
        preferred_element_type=jnp.float32,
    ).astype(jnp.bfloat16)
    start_state = (
        jnp.full((local_heads, row_count), -jnp.inf, jnp.float32),
        jnp.zeros((local_heads, row_count), jnp.float32),
        jnp.zeros((local_heads, row_count, HEAD_DIM), jnp.float32),
    )
    query_heads = queries.reshape(row_count, local_heads, HEAD_DIM)
    final_state = absorb(
        start_state,
        query_heads,
        lax.all_gather(enc_keys, "blk", axis=0, tiled=True),
        lax.all_gather(enc_values, "blk", axis=0, tiled=True),
    )
    context = final_state[2] / final_state[1][:, :, None]
    context = jnp.transpose(context, (1, 0, 2)).reshape(row_count, columns).astype(jnp.bfloat16)
    out_full = lax.all_gather(w_out_t, "blk", axis=0, tiled=True)
    return lax.psum_scatter(
        lax.dot_general(
            context, out_full, (((1,), (1,)), ((), ())), preferred_element_type=jnp.float32
        ),
        "fsdp",
        scatter_dimension=0,
        tiled=True,
    ).astype(jnp.bfloat16)


def solution(mesh):
    in_specs = (
        P("blk", "fsdp"),
        P("blk", "fsdp"),
        P("blk", "fsdp"),
        P("blk", "fsdp"),
        P("blk", "fsdp"),
    )
    out_specs = P(("blk", "fsdp"), None)
    return jax.shard_map(shards, mesh=mesh, in_specs=in_specs, out_specs=out_specs, check_vma=False)
```

profile of v0, /device:TPU:8, one launch (start us, length us, event | category | flops | bytes accessed | tf_op | source)
XLA Modules:
  0.0 624.3 jit_solution(10942586508582458863)
XLA Ops:
  6.5 0.7 all-gather.6.cloned.1.call-update
  7.3 0.0 all-gather.8.cloned.1.call-start
  7.3 0.7 all-gather.8.cloned.1.call-update
  8.0 0.0 all-gather.10.cloned.1.call-start
  8.1 0.7 all-gather.10.cloned.1.call-update
  8.7 0.0 all-gather.12.cloned.1.call-start
  8.8 0.5 all-gather.12.cloned.1.call-update
  9.3 0.0 all-gather.14.cloned.1.call-start
  9.4 0.5 all-gather.14.cloned.1.call-update
  9.9 0.0 reduce-scatter.2.cloned.1.call-start
  10.0 110.0 %all-gather.6.cloned.1.call-done = bf16[256,4096]{1,0:T(8,128)(2,1)} async-done(((bf16[256,256]{1,0:T(8,128)(2,1)}), bf16[256,4096]{1,0:T(8,128)(2,1)}) %all-gather.6.cloned.1.call-update) | async-done | bytes 2097168 | tf_op jit(solution)/shard_map/all_gather | solution.py:38
  120.0 59.1 %all-gather.8.cloned.1.call-done = bf16[4096,256]{1,0:T(8,128)(2,1)} async-done(((bf16[128,256]{1,0:T(8,128)(2,1)}), bf16[4096,256]{1,0:T(8,128)(2,1)}) %all-gather.8.cloned.1.call-update) | async-done | bytes 2097168 | tf_op jit(solution)/shard_map/all_gather | solution.py:33
  179.0 3.1 convolution_convert_fusion
  182.2 63.7 %all-gather.10.cloned.1.call-done = bf16[8192,256]{1,0:T(8,128)(2,1)} async-done(((bf16[256,256]{1,0:T(8,128)(2,1)}), bf16[8192,256]{1,0:T(8,128)(2,1)}) %all-gather.10.cloned.1.call-update) | async-done | bytes 4194320 | tf_op jit(solution)/shard_map/all_gather | solution.py:51
  245.9 6.4 %copy.6 = bf16[8192,256]{0,1:T(8,128)(2,1)} copy(bf16[8192,256]{1,0:T(8,128)(2,1)} %all-gather.10.cloned.1.call-done) | data formatting | bytes 8388608 | tf_op jit(solution)/shard_map/all_gather | solution.py:51
  252.3 15.5 %multiply_reduce_fusion = (f32[4,256]{1,0:T(4,128)S(1)}, f32[4,256,8192]{2,1,0:T(8,128)}) fusion(bf16[256,4,64]{0,2,1:T(8,128)(2,1)S(1)} %bitcast.27, bf16[8192,4,64]{0,2,1:T(8,128)(2,1)} %bitcast.26), kind=kOutput, calls=%fused_computation.1 | convolution fusion | flops 1090518016 | bytes 37883904 | tf_op jit(solution)/shard_map/qhd,khd->hqk/dot_general | solution.py:16
  267.8 44.6 %all-gather.12.cloned.1.call-done = bf16[8192,256]{1,0:T(8,128)(2,1)} async-done(((bf16[256,256]{1,0:T(8,128)(2,1)}), bf16[8192,256]{1,0:T(8,128)(2,1)}) %all-gather.12.cloned.1.call-update) | async-done | bytes 4194320 | tf_op jit(solution)/shard_map/all_gather | solution.py:52
  312.4 6.4 %copy.7 = bf16[8192,256]{0,1:T(8,128)(2,1)} copy(bf16[8192,256]{1,0:T(8,128)(2,1)} %all-gather.12.cloned.1.call-done) | data formatting | bytes 8388608 | tf_op jit(solution)/shard_map/all_gather | solution.py:52
  318.8 14.1 %fusion = f32[4,256]{1,0:T(4,128)S(1)} fusion(f32[4,256,8192]{2,1,0:T(8,128)} %get-tuple-element.6, f32[4,256]{1,0:T(4,128)S(1)} %get-tuple-element.5), kind=kLoop, calls=%fused_computation.2 | loop fusion | flops 25164800 | bytes 33562624 | tf_op jit(solution)/shard_map/reduce_sum | solution.py:22
  332.9 15.5 %fusion.13 = bf16[256,4,64]{0,2,1:T(8,128)(2,1)S(1)} fusion(bf16[8192,4,64]{0,2,1:T(8,128)(2,1)} %bitcast.25, f32[4,256,8192]{2,1,0:T(8,128)} %get-tuple-element.6, f32[4,256]{1,0:T(4,128)S(1)} %get-tuple-element.5, f32[256,4]{0,1:T(4,128)S(1)} %bitcast_add_fusion, f32[256,4]{0,1:T(4,128)S(1)} %multiply_bitcast_fusion), kind=kOutput, calls=%fused_computation.9 | convolution fusion | flops 1099104256 | bytes 37892096 | tf_op jit(solution)/shard_map/hqk,khd->hqd/dot_general | solution.py:23
  348.5 27.8 %all-gather.14.cloned.1.call-done = bf16[4096,256]{1,0:T(8,128)(2,1)} async-done(((bf16[128,256]{1,0:T(8,128)(2,1)}), bf16[4096,256]{1,0:T(8,128)(2,1)}) %all-gather.14.cloned.1.call-update) | async-done | bytes 2097168 | tf_op jit(solution)/shard_map/all_gather | solution.py:56
  376.3 4.3 fusion.17
  380.6 235.3 %reduce-scatter.2.cloned.1.call-done = f32[16,4096]{1,0:T(8,128)} async-done(((f32[256,4096]{1,0:T(8,128)}), f32[16,4096]{1,0:T(8,128)}) %reduce-scatter.2.cloned.1.call-update) | async-done | bytes 262160 | tf_op jit(solution)/shard_map/reduce_scatter | solution.py:57
  615.8 1.6 convert_element_type.19
  (4 shorter events, 0.0 us)
Async XLA Ops:
  6.5 113.4 %all-gather.6.cloned.1.call-start = ((), (), s32[]{:S(2)}) async-start(), calls=%async_computation.1 | async-start | bytes 2228224 | tf_op jit(solution)/shard_map/all_gather | solution.py:38
  7.3 171.8 %all-gather.8.cloned.1.call-start = ((), (), s32[]{:S(2)}) async-start(), calls=%async_computation.2 | async-start | bytes 2162688 | tf_op jit(solution)/shard_map/all_gather | solution.py:33
  8.0 237.8 %all-gather.10.cloned.1.call-start = ((), (), s32[]{:S(2)}) async-start(), calls=%async_computation.3 | async-start | bytes 4325376 | tf_op jit(solution)/shard_map/all_gather | solution.py:51
  8.7 303.7 %all-gather.12.cloned.1.call-start = ((), (), s32[]{:S(2)}) async-start(), calls=%async_computation.4 | async-start | bytes 4325376 | tf_op jit(solution)/shard_map/all_gather | solution.py:52
  9.3 366.9 %all-gather.14.cloned.1.call-start = ((), (), s32[]{:S(2)}) async-start(), calls=%async_computation.5 | async-start | bytes 2162688 | tf_op jit(solution)/shard_map/all_gather | solution.py:56
  9.9 605.9 %reduce-scatter.2.cloned.1.call-start = ((), (), s32[]{:S(2)}) async-start(), calls=%async_computation.6 | async-start | bytes 4456448 | tf_op jit(solution)/shard_map/reduce_scatter | solution.py:57
Sparse Core Ops, SparseCore 0:
  10.4 109.5 all-gather.5
  122.1 56.8 all-gather.7
  181.2 64.6 all-gather.9
  247.9 64.5 all-gather.11
  314.4 61.7 all-gather.13
  380.7 235.0 reduce-scatter.1
where the time goes:
time: 625 us; the launch traced here: 624 us
  waiting for transfers between devices  544 us (87%)
  matrix products  38.5 us (6%)
  other arithmetic  15.7 us (3%)
  between operations  13.5 us (2%)
  local copies, waits for them, and re-layouts  12.8 us (2%)
    reduce_scatter x1, waiting for transfers between devices, shards(): lax.psum_scatter(lax.dot_general(context, out_full, (((1,), (1,)), ((), (...  235 us
    all_gather x1, waiting for transfers between devices, shards(): lax.all_gather(decoder_states, 'fsdp', axis=1, tiled=True)  110 us
    all_gather x1, waiting for transfers between devices, shards(): lax.all_gather(enc_keys, 'blk', axis=0, tiled=True)  63.7 us
    all_gather x1, waiting for transfers between devices, shards(): query_full = lax.all_gather(w_query, 'blk', axis=0, tiled=True)  59.1 us
    all_gather x1, waiting for transfers between devices, shards(): lax.all_gather(enc_values, 'blk', axis=0, tiled=True)  44.6 us
    all_gather x1, waiting for transfers between devices, shards(): out_full = lax.all_gather(w_out_t, 'blk', axis=0, tiled=True)  27.8 us
    dot_general x1, matrix products, absorb(): jnp.einsum('hqk,khd->hqd', probability.astype(jnp.bfloat16), value_heads,...  15.5 us
    dot_general x1, matrix products, absorb(): jnp.einsum('qhd,khd->hqk', query_heads, key_heads, preferred_element_type...  15.5 us
  transfers between devices with their start and end apart: 6, of which 6 were waited for; matrix products, arithmetic and copies ran while one was open for 10% of the time, Pallas kernels for 0%

commit v1 on v0

v1 whole, which is shorter than its diff:
```python
import functools
import math

import jax
import jax.numpy as jnp
from jax import lax
from jax.experimental import pallas as pl
from jax.experimental.pallas import tpu as pltpu
from jax.sharding import PartitionSpec as P

HEAD_DIM = 64
NX, NY, NC, NZ, NH = 4, 4, 2, 8, 2
MESH = pl.DeviceIdType.MESH
BF16, F32 = jnp.bfloat16, jnp.float32
VMEM = pltpu.VMEM


def place():
    b = lax.axis_index("blk")
    f = lax.axis_index("fsdp")
    x = lax.div(b, NY * NC)
    y = lax.rem(lax.div(b, NC), NY)
    c = lax.rem(b, NC)
    return x, y, c, lax.div(f, NH), lax.rem(f, NH)


def blk_id(x, y, c):
    return {"blk": x * (NY * NC) + y * NC + c}


def fsdp_id(z, h):
    return {"fsdp": z * NH + h}


def greet(peers):
    barrier = pltpu.get_barrier_semaphore()
    for peer in peers:
        pl.semaphore_signal(barrier, inc=1, device_id=peer, device_id_type=MESH)
    pl.semaphore_wait(barrier, len(peers))


class Links:
    def __init__(self, send_sem, recv_sem):
        self.send_sem, self.recv_sem, self.copies = send_sem, recv_sem, []

    def send(self, src, dst, peer):
        k = len(self.copies)
        copy = pltpu.make_async_remote_copy(
            src_ref=src, dst_ref=dst, send_sem=self.send_sem.at[k],
            recv_sem=self.recv_sem.at[k], device_id=peer, device_id_type=MESH,
        )
        copy.start()
        self.copies.append(copy)
        return copy

    def drain(self):
        for copy in self.copies:
            copy.wait_send()


def gather_kernel(x_ref, wq_ref, wo_ref, kv_ref, xg, wqg, wog, kvg, local_sem, send_sem, recv_sem):
    x, y, c, z, h = place()
    xr, xl = lax.rem(x + 1, NX), lax.rem(x + NX - 1, NX)
    zr, zl = lax.rem(z + 1, NZ), lax.rem(z + NZ - 1, NZ)
    ys = [lax.rem(y + r, NY) for r in (1, 2, 3)]
    right, left, other = blk_id(xr, y, c), blk_id(xl, y, c), blk_id(x, y, 1 - c)
    up, down, far = fsdp_id(zr, h), fsdp_id(zl, h), fsdp_id(z, 1 - h)
    greet([right, left, other, up, down, far] + [blk_id(x, yp, c) for yp in ys])
    net = Links(send_sem, recv_sem)

    own = [
        pltpu.make_async_copy(x_ref, xg.at[z, h], local_sem.at[0]),
        pltpu.make_async_copy(wq_ref, wqg.at[x, y, c], local_sem.at[1]),
        pltpu.make_async_copy(kv_ref.at[y], kvg.at[x, y, c], local_sem.at[2]),
        pltpu.make_async_copy(wo_ref, wog.at[x, y, c], local_sem.at[3]),
    ]
    for copy in own:
        copy.start()
    pair = net.send(x_ref, xg.at[z, h], far)
    columns = []
    for buf, piece in ((wqg, lambda yp: wq_ref), (kvg, lambda yp: kv_ref.at[yp]), (wog, lambda yp: wo_ref)):
        columns.append([net.send(piece(yp), buf.at[x, y, c], blk_id(x, yp, c)) for yp in ys])
    for copy in own:
        copy.wait()

    def z_step(s):
        a, b = lax.rem(z + NZ - s, NZ), lax.rem(z + s, NZ)
        if s < 3:
            return (net.send(xg.at[a], xg.at[a], up), net.send(xg.at[b], xg.at[b], down))
        return (net.send(xg.at[a, 0], xg.at[a, 0], up), net.send(xg.at[b, 1], xg.at[b, 1], down))

    def x_first(buf, arrivals):
        for copy in arrivals:
            copy.wait_recv()
        block = buf.at[x, :, c]
        return (net.send(block, block, right), net.send(block, block, left))

    def x_second(buf, arrivals):
        for copy in arrivals:
            copy.wait_recv()
        a, b = buf.at[xl, pl.ds(0, 2), c], buf.at[xr, pl.ds(2, 2), c]
        return (net.send(a, a, right), net.send(b, b, left))

    def core_step(buf, arrivals):
        for copy in arrivals:
            copy.wait_recv()
        half = buf.at[:, :, c]
        return net.send(half, half, other)

    def z_wait(arrivals):
        for copy in arrivals:
            copy.wait_recv()

    bufs = (wqg, kvg, wog)
    pair.wait_recv()
    zc = z_step(0)
    first = [x_first(buf, got) for buf, got in zip(bufs, columns)]
    z_wait(zc)
    zc = z_step(1)
    second = [x_second(wqg, first[0])]
    z_wait(zc)
    zc = z_step(2)
    last = [core_step(wqg, second[0])]
    second.append(x_second(kvg, first[1]))
    z_wait(zc)
    zc = z_step(3)
    last.append(core_step(kvg, second[1]))
    second.append(x_second(wog, first[2]))
    last.append(core_step(wog, second[2]))
    z_wait(zc)
    z_wait(last)
    net.drain()


def gather(x, wq, wo, kv):
    rows, cols = x.shape
    depth = wq.shape[0]
    copies = 1 + 9 + 8 + 12 + 3
    any_spec = pl.BlockSpec(memory_space=pl.ANY)
    return pl.pallas_call(
        gather_kernel,
        name="gather_inputs",
        out_shape=(
            jax.ShapeDtypeStruct((NZ, NH, rows, cols), BF16),
            jax.ShapeDtypeStruct((NX, NY, NC, depth, cols), BF16),
            jax.ShapeDtypeStruct((NX, NY, NC, depth, cols), BF16),
            jax.ShapeDtypeStruct((NX, NY, NC) + kv.shape[1:], BF16),
        ),
        in_specs=[pl.BlockSpec(memory_space=VMEM)] * 4,
        out_specs=(any_spec,) * 4,
        scratch_shapes=[
            pltpu.SemaphoreType.DMA((4,)),
            pltpu.SemaphoreType.DMA((copies,)),
            pltpu.SemaphoreType.DMA((copies,)),
        ],
        compiler_params=pltpu.CompilerParams(collective_id=0, has_side_effects=True),
    )(x, wq, wo, kv)


def swap_kernel(src, dst, local_sem, send_sem, recv_sem):
    x, y, c, z, h = place()
    ys = [lax.rem(y + r, NY) for r in (1, 2, 3)]
    peers = [blk_id(x, yp, c) for yp in ys]
    greet(peers)
    net = Links(send_sem, recv_sem)
    own = pltpu.make_async_copy(src.at[y], dst.at[y], local_sem)
    own.start()
    got = [net.send(src.at[yp], dst.at[y], peer) for yp, peer in zip(ys, peers)]
    own.wait()
    for copy in got:
        copy.wait_recv()
    net.drain()


def swap(blocks, name, collective_id):
    return pl.pallas_call(
        swap_kernel,
        name=name,
        out_shape=jax.ShapeDtypeStruct(blocks.shape, blocks.dtype),
        in_specs=[pl.BlockSpec(memory_space=VMEM)],
        out_specs=pl.BlockSpec(memory_space=VMEM),
        scratch_shapes=[
            pltpu.SemaphoreType.DMA,
            pltpu.SemaphoreType.DMA((3,)),
            pltpu.SemaphoreType.DMA((3,)),
        ],
        compiler_params=pltpu.CompilerParams(collective_id=collective_id, has_side_effects=True),
    )(blocks)


def query_kernel(x_ref, w_ref, q_ref, total):
    step = pl.program_id(0)

    @pl.when(step == 0)
    def _():
        total[...] = jnp.zeros_like(total)

    for k in range(x_ref.shape[0]):
        total[...] += jnp.dot(x_ref[k], w_ref[k], preferred_element_type=F32)

    @pl.when(step == pl.num_programs(0) - 1)
    def _():
        q = total[...].astype(BF16)
        zero = jnp.zeros((q.shape[0], HEAD_DIM), BF16)
        for j in range(q_ref.shape[0]):
            q_ref[j] = jnp.concatenate([q[:, j * HEAD_DIM:(j + 1) * HEAD_DIM], zero], axis=1)


def project_queries(xg, wq):
    parts, rows, cols = xg.shape
    n = wq.shape[2]
    heads = n // HEAD_DIM
    return pl.pallas_call(
        query_kernel,
        name="project_queries",
        grid=(4,),
        out_shape=jax.ShapeDtypeStruct((heads, rows, 2 * HEAD_DIM), BF16),
        in_specs=[
            pl.BlockSpec((parts // 4, rows, cols), lambda i: (i, 0, 0)),
            pl.BlockSpec((parts // 4, cols, n), lambda i: (i, 0, 0)),
        ],
        out_specs=pl.BlockSpec((heads, rows, 2 * HEAD_DIM), lambda i: (0, 0, 0)),
        scratch_shapes=[VMEM((rows, n), F32)],
    )(xg, wq)


def attend_kernel(q_ref, kv_ref, o_ref, ones_v):
    keys = kv_ref.shape[0]
    chunk = 1024
    factor = 1.0 / (math.sqrt(HEAD_DIM) * math.log(2.0))

    @pl.when(pl.program_id(0) == 0)
    def _():
        lane = lax.broadcasted_iota(jnp.int32, (chunk, 2 * HEAD_DIM), 1)

        @pl.loop(0, keys // chunk)
        def _(i):
            at = pl.ds(pl.multiple_of(i * chunk, chunk), chunk)
            v = kv_ref[at, :].astype(F32)
            ones_v[at, :] = jnp.where(lane < HEAD_DIM, 1.0, v).astype(BF16)

    q = q_ref[...]
    rows = q.shape[0]

    def body(i, state):
        top, total = state
        at = pl.ds(pl.multiple_of(i * chunk, chunk), chunk)
        s = lax.dot_general(
            q, kv_ref[at, :], (((1,), (1,)), ((), ())), preferred_element_type=F32
        )
        new_top = jnp.maximum(top, jnp.max(s, axis=1, keepdims=True))
        p = jnp.exp2((s - new_top) * factor)
        rescale = jnp.exp2((top - new_top) * factor)
        total = total * rescale + jnp.dot(
            p.astype(BF16), ones_v[at, :], preferred_element_type=F32
        )
        return new_top, total

    start = (jnp.full((rows, 1), -jnp.inf, F32), jnp.zeros((rows, 2 * HEAD_DIM), F32))
    _, total = lax.fori_loop(0, keys // chunk, body, start, unroll=2)
    context = total[:, HEAD_DIM:] / total[:, :HEAD_DIM]
    o_ref[...] = jnp.concatenate([context, context], axis=1).astype(BF16)


def attend(q, kv):
    rows, wide = q.shape
    tile = 256
    return pl.pallas_call(
        attend_kernel,
        name="attend",
        grid=(rows // tile,),
        out_shape=jax.ShapeDtypeStruct((rows, wide), BF16),
        in_specs=[
            pl.BlockSpec((tile, wide), lambda i: (i, 0)),
            pl.BlockSpec(kv.shape, lambda i: (0, 0)),
        ],
        out_specs=pl.BlockSpec((tile, wide), lambda i: (i, 0)),
        scratch_shapes=[VMEM(kv.shape, BF16)],
    )(q, kv)


def project_kernel(c_ref, w_ref, o_ref):
    context = jnp.concatenate([c_ref[j][:, :HEAD_DIM] for j in range(c_ref.shape[0])], axis=1)
    o_ref[...] = lax.dot_general(
        context, w_ref[...], (((1,), (1,)), ((), ())), preferred_element_type=F32
    ).astype(BF16)


def project_out(context, wo):
    heads, rows, wide = context.shape
    out, cols = wo.shape
    tile = 1024
    return pl.pallas_call(
        project_kernel,
        name="project_out",
        grid=(out // tile,),
        out_shape=jax.ShapeDtypeStruct((rows, out), BF16),
        in_specs=[
            pl.BlockSpec((heads, rows, wide), lambda i: (0, 0, 0)),
            pl.BlockSpec((tile, cols), lambda i: (i, 0)),
        ],
        out_specs=pl.BlockSpec((rows, tile), lambda i: (0, i)),
    )(context, wo)


def reduce_kernel(p_ref, o_ref, half_r, half_l, in_r, in_l, out_r, out_l, total, far_out, far_in,
                  send_sem, recv_sem):
    x, y, c, z, h = place()
    up, down = fsdp_id(lax.rem(z + 1, NZ), h), fsdp_id(lax.rem(z + NZ - 1, NZ), h)
    far = fsdp_id(z, 1 - h)
    greet([up, down, far])
    net = Links(send_sem, recv_sem)
    opposite = lax.rem(z + 4, NZ)
    r = net.send(p_ref.at[opposite, 0], half_r, up)
    l = net.send(p_ref.at[opposite, 1], half_l, down)
    for s in range(3):
        ahead, behind = lax.rem(z + 3 - s, NZ), lax.rem(z + NZ - 3 + s, NZ)
        r.wait_recv()
        if s == 0:
            out_r[0, 0] = (p_ref[ahead, 0].astype(F32) + half_r[...].astype(F32)).astype(BF16)
            out_r[0, 1] = p_ref[ahead, 1]
        else:
            out_r[s] = (p_ref[ahead].astype(F32) + in_r[s - 1].astype(F32)).astype(BF16)
        r = net.send(out_r.at[s], in_r.at[s], up)
        l.wait_recv()
        if s == 0:
            out_l[0, 0] = p_ref[behind, 0]
            out_l[0, 1] = (p_ref[behind, 1].astype(F32) + half_l[...].astype(F32)).astype(BF16)
        else:
            out_l[s] = (p_ref[behind].astype(F32) + in_l[s - 1].astype(F32)).astype(BF16)
        l = net.send(out_l.at[s], in_l.at[s], down)
    r.wait_recv()
    l.wait_recv()
    total[...] = p_ref[z].astype(F32) + in_r[2].astype(F32) + in_l[2].astype(F32)
    far_out[...] = total[1 - h].astype(BF16)
    w = net.send(far_out, far_in, far)
    w.wait_recv()
    o_ref[...] = (total[h] + far_in[...].astype(F32)).astype(BF16)
    net.drain()


def reduce_rows(partial):
    one = partial.shape[2:]
    two = partial.shape[1:]
    return pl.pallas_call(
        reduce_kernel,
        name="reduce_rows",
        out_shape=jax.ShapeDtypeStruct(one, BF16),
        in_specs=[pl.BlockSpec(memory_space=VMEM)],
        out_specs=pl.BlockSpec(memory_space=VMEM),
        scratch_shapes=[
            VMEM(one, BF16), VMEM(one, BF16),
            VMEM((3,) + two, BF16), VMEM((3,) + two, BF16),
            VMEM((3,) + two, BF16), VMEM((3,) + two, BF16),
            VMEM(two, F32), VMEM(one, BF16), VMEM(one, BF16),
            pltpu.SemaphoreType.DMA((9,)),
            pltpu.SemaphoreType.DMA((9,)),
        ],
        compiler_params=pltpu.CompilerParams(collective_id=3, has_side_effects=True),
    )(partial)


def shards(decoder_states, w_query, w_out_t, enc_keys, enc_values):
    rows, cols = decoder_states.shape
    heads = cols // HEAD_DIM
    keys = enc_keys.reshape(-1, heads, HEAD_DIM)
    values = enc_values.reshape(-1, heads, HEAD_DIM)
    kv = jnp.transpose(jnp.concatenate([keys, values], axis=2), (1, 0, 2))
    xg, wqg, wog, kvg = gather(decoder_states, w_query, w_out_t, kv)
    q = project_queries(xg.reshape(NZ * NH, rows, cols), wqg.reshape(NZ * NH, cols, cols))
    q = swap(q, "swap_queries", 1)
    context = attend(q.reshape(NY * rows, 2 * HEAD_DIM), kvg.reshape(-1, 2 * HEAD_DIM))
    context = swap(context.reshape(NY, rows, 2 * HEAD_DIM), "swap_context", 2)
    partial = project_out(context, wog.reshape(-1, cols))
    return reduce_rows(partial.reshape(NZ, NH, rows // (NZ * NH), partial.shape[1]))


def solution(mesh):
    spec = P("blk", "fsdp")
    return jax.shard_map(
        shards, mesh=mesh, in_specs=(spec,) * 5,
        out_specs=P(("blk", "fsdp"), None), check_vma=False,
    )
```

time: 625 us -> 163 us (0.26)
  the two profiles are of different devices: /device:TPU:8 before, /device:TPU:64 now
where the time goes in v1:
time: 163 us; the launch traced here: 162 us
  Pallas kernels  158 us (97%)
  local copies, waits for them, and re-layouts  3.92 us (2%)
    pallas_call x1, Pallas kernels, gather(): pl.pallas_call(gather_kernel, name='gather_inputs', out_shape=(jax.ShapeD...  60.5 us
    pallas_call x1, Pallas kernels, reduce_rows(): pl.pallas_call(reduce_kernel, name='reduce_rows', out_shape=jax.ShapeDtyp...  45.2 us
    pallas_call x2, Pallas kernels, swap(): pl.pallas_call(swap_kernel, name=name, out_shape=jax.ShapeDtypeStruct(blo...  22.4 us
    pallas_call x1, Pallas kernels, attend(): pl.pallas_call(attend_kernel, name='attend', grid=(rows // tile,), out_sh...  20.5 us
    pallas_call x1, Pallas kernels, project_out(): pl.pallas_call(project_kernel, name='project_out', grid=(out // tile,), o...  4.62 us
    pallas_call x1, Pallas kernels, project_queries(): pl.pallas_call(query_kernel, name='project_queries', grid=(4,), out_shape...  4.29 us
    unnamed x3, local copies, waits for them, and re-layouts  3.57 us

profile of v1, /device:TPU:64, one launch (start us, length us, event | category | flops | bytes accessed | tf_op | source)
XLA Modules:
  0.0 162.4 jit_solution(10650130873167714678)
XLA Ops:
  0.0 1.0 copy.6
  1.0 0.2 copy.8
  1.2 1.0 copy.7
  2.2 0.2 copy.9
  2.4 0.9 maximum_bitcast_fusion.kv_ref
  3.3 60.5 %gather_inputs.1 = (bf16[8,2,256,256]{3,2,1,0:T(8,128)(2,1)}, bf16[4,4,2,128,256]{4,3,2,1,0:T(8,128)(2,1)}, bf16[4,4,2,128,256]{4,3,2,1,0:T(8,128)(2,1)}, bf16[4,4,2,256,128]{4,3,2,1,0:T(8,128)(2,1)}) custom-call(bf16[256,256]{1,0:T(8,128)(2,1)} %x_ref.1, bf16[128,256]{1,0:T(8,128)(2,1)} %wq_ref.1, bf16[128,256]{1,0:T(8,128)(2,1)} %wo_ref.1, ...), custom_call_target="tpu_custom_call" | custom-call | tf_op jit(solution)/shard_map/gather_inputs/pallas_call | solution.py:140
  63.8 4.3 %project_queries.1.src = bf16[4,256,128]{2,1,0:T(8,128)(2,1)} custom-call(bf16[16,256,256]{2,1,0:T(8,128)(2,1)} %bitcast.14, bf16[16,256,256]{2,1,0:T(8,128)(2,1)} %bitcast.15), custom_call_target="tpu_custom_call" | custom-call | tf_op jit(solution)/shard_map/project_queries/pallas_call | solution.py:213
  68.1 11.8 %swap_queries.1 = bf16[4,256,128]{2,1,0:T(8,128)(2,1)} custom-call(bf16[4,256,128]{2,1,0:T(8,128)(2,1)} %project_queries.1.src), custom_call_target="tpu_custom_call" | custom-call | tf_op jit(solution)/shard_map/swap_queries/pallas_call | solution.py:176
  79.9 20.5 %attend.1 = bf16[1024,128]{1,0:T(8,128)(2,1)} custom-call(bf16[1024,128]{1,0:T(8,128)(2,1)} %bitcast.16, bf16[8192,128]{1,0:T(8,128)(2,1)} %bitcast.12), custom_call_target="tpu_custom_call" | custom-call | tf_op jit(solution)/shard_map/attend/pallas_call | solution.py:268
  100.4 10.5 %swap_context.1.c_ref = bf16[4,256,128]{2,1,0:T(8,128)(2,1)} custom-call(bf16[4,256,128]{2,1,0:T(8,128)(2,1)} %bitcast.17), custom_call_target="tpu_custom_call" | custom-call | tf_op jit(solution)/shard_map/swap_context/pallas_call | solution.py:176
  111.0 4.6 %project_out.1 = bf16[256,4096]{1,0:T(8,128)(2,1)} custom-call(bf16[4,256,128]{2,1,0:T(8,128)(2,1)} %swap_context.1.c_ref, bf16[4096,256]{1,0:T(8,128)(2,1)} %bitcast.13), custom_call_target="tpu_custom_call" | custom-call | tf_op jit(solution)/shard_map/project_out/pallas_call | solution.py:293
  115.6 45.2 %reduce_rows.1 = bf16[16,4096]{1,0:T(8,128)(2,1)} custom-call(bf16[8,2,16,4096]{3,2,1,0:T(8,128)(2,1)} %bitcast.11), custom_call_target="tpu_custom_call" | custom-call | tf_op jit(solution)/shard_map/reduce_rows/pallas_call | solution.py:345
  160.8 1.6 copy.11

commit v2 on v0

v2 whole, which is shorter than its diff:
```python
import math

import jax
import jax.numpy as jnp
from jax import lax
from jax.experimental import pallas as pl
from jax.experimental.pallas import tpu as pltpu
from jax.sharding import PartitionSpec as P

HEAD_DIM = 64
NX, NY, NC, NZ, NH = 4, 4, 2, 8, 2
MESH = pl.DeviceIdType.MESH
BF16, F32 = jnp.bfloat16, jnp.float32
VMEM = pltpu.VMEM


def place():
    b = lax.axis_index("blk")
    f = lax.axis_index("fsdp")
    x = lax.div(b, NY * NC)
    y = lax.rem(lax.div(b, NC), NY)
    c = lax.rem(b, NC)
    return x, y, c, lax.div(f, NH), lax.rem(f, NH)


def blk_id(x, y, c):
    return {"blk": x * (NY * NC) + y * NC + c}


def fsdp_id(z, h):
    return {"fsdp": z * NH + h}


def greet(peers):
    barrier = pltpu.get_barrier_semaphore()
    for peer in peers:
        pl.semaphore_signal(barrier, inc=1, device_id=peer, device_id_type=MESH)
    return lambda: pl.semaphore_wait(barrier, len(peers))


def arrive(copies):
    for copy in copies:
        copy.wait_recv()


class Links:
    def __init__(self, send_sem, recv_sem):
        self.send_sem, self.recv_sem, self.copies = send_sem, recv_sem, []

    def send(self, src, dst, peer):
        k = len(self.copies)
        copy = pltpu.make_async_remote_copy(
            src_ref=src, dst_ref=dst, send_sem=self.send_sem.at[k],
            recv_sem=self.recv_sem.at[k], device_id=peer, device_id_type=MESH,
        )
        copy.start()
        self.copies.append(copy)
        return copy

    def drain(self):
        for copy in self.copies:
            copy.wait_send()


class Spread:
    def __init__(self, net, buf, x, y, c):
        self.net, self.buf, self.c, self.x = net, buf, c, x
        self.xs = [lax.rem(x + r, NX) for r in (1, 2, 3)]
        self.right, self.left = blk_id(self.xs[0], y, c), blk_id(self.xs[2], y, c)
        self.other = blk_id(x, y, 1 - c)
        self.cores = []

    def to_core(self, *xs):
        for at in xs:
            block = self.buf.at[at, :, self.c]
            self.cores.append(self.net.send(block, block, self.other))

    def first(self, arrivals):
        arrive(arrivals)
        block = self.buf.at[self.x, :, self.c]
        self.hop = (self.net.send(block, block, self.right), self.net.send(block, block, self.left))
        self.to_core(self.x)

    def second(self):
        arrive(self.hop)
        a = self.buf.at[self.xs[2], pl.ds(0, 2), self.c]
        b = self.buf.at[self.xs[0], pl.ds(2, 2), self.c]
        self.hop = (self.net.send(a, a, self.right), self.net.send(b, b, self.left))
        self.to_core(self.xs[0], self.xs[2])

    def third(self):
        arrive(self.hop)
        self.to_core(self.xs[1])

    def finish(self):
        arrive(self.cores)


def queries_kernel(x_ref, wq_ref, k_ref, v_ref, q_ref, kvg, xg, wqg, kv, qs, local_sem, send_sem, recv_sem):
    x, y, c, z, h = place()
    ys = [lax.rem(y + r, NY) for r in (1, 2, 3)]
    column = [blk_id(x, yp, c) for yp in ys]
    up, down = fsdp_id(lax.rem(z + 1, NZ), h), fsdp_id(lax.rem(z + NZ - 1, NZ), h)
    far = fsdp_id(z, 1 - h)
    net = Links(send_sem, recv_sem)
    weights, pairs = Spread(net, wqg, x, y, c), Spread(net, kvg, x, y, c)
    ready = greet([weights.right, weights.left, weights.other, up, down, far] + column)
    for j in range(NY):
        cols = slice(j * HEAD_DIM, (j + 1) * HEAD_DIM)
        kv[j] = jnp.concatenate([k_ref[:, cols], v_ref[:, cols]], axis=1)
    ready()

    def ring(s, part, is_own, both):
        a, b = lax.rem(z + NZ - s, NZ), lax.rem(z + s, NZ)
        sent = []
        if both != "down":
            src = x_ref if is_own and s == 0 else xg.at[a, part]
            sent.append(net.send(src, xg.at[a, part], up))
        if both != "up":
            src = x_ref if is_own and s == 0 else xg.at[b, part]
            sent.append(net.send(src, xg.at[b, part], down))
        return sent

    pair = net.send(x_ref, xg.at[z, h], far)
    own_ring = ring(0, h, True, "both")
    own = [
        pltpu.make_async_copy(x_ref, xg.at[z, h], local_sem.at[0]),
        pltpu.make_async_copy(wq_ref, wqg.at[x, y, c], local_sem.at[1]),
        pltpu.make_async_copy(kv.at[y], kvg.at[x, y, c], local_sem.at[2]),
    ]
    for copy in own:
        copy.start()
    w_col = [net.send(wq_ref, wqg.at[x, y, c], to) for to in column]
    kv_col = [net.send(kv.at[yp], kvg.at[x, y, c], to) for yp, to in zip(ys, column)]
    for copy in own:
        copy.wait()
    arrive(own_ring)
    own_ring = ring(1, h, True, "both")
    weights.first(w_col)
    arrive(own_ring)
    own_ring = ring(2, h, True, "both")
    arrive([pair])
    far_ring = ring(0, 1 - h, False, "both")
    pairs.first(kv_col)
    arrive(own_ring)
    own_ring = ring(3, h, True, "up")
    weights.second()
    arrive(far_ring)
    far_ring = ring(1, 1 - h, False, "both")
    weights.third()
    pairs.second()
    arrive(far_ring)
    far_ring = ring(2, 1 - h, False, "both")
    pairs.third()
    arrive(own_ring)
    arrive(far_ring)
    far_ring = ring(3, 1 - h, False, "down")
    weights.finish()
    arrive(far_ring)

    total = None
    for f in range(NZ * NH):
        w = wqg[f // NY, f % NY]
        part = jnp.dot(
            xg[f // NH, f % NH], w.reshape(-1, w.shape[-1]), preferred_element_type=F32
        )
        total = part if total is None else total + part
    q = total.astype(BF16)
    zero = jnp.zeros((q.shape[0], HEAD_DIM), BF16)
    for j in range(NY):
        qs[j] = jnp.concatenate([q[:, j * HEAD_DIM:(j + 1) * HEAD_DIM], zero], axis=1)
    swaps = [net.send(qs.at[yp], q_ref.at[y], to) for yp, to in zip(ys, column)]
    q_ref[y] = qs[y]
    pairs.finish()
    arrive(swaps)
    net.drain()


def queries_and_pairs(x, wq, k, v):
    rows, cols = x.shape
    depth = wq.shape[0]
    heads = (NY, rows, 2 * HEAD_DIM)
    vmem = pl.BlockSpec(memory_space=VMEM)
    return pl.pallas_call(
        queries_kernel,
        name="queries_and_pairs",
        out_shape=(
            jax.ShapeDtypeStruct(heads, BF16),
            jax.ShapeDtypeStruct((NX, NY, NC, rows, 2 * HEAD_DIM), BF16),
        ),
        in_specs=[vmem] * 4,
        out_specs=(vmem, pl.BlockSpec(memory_space=pl.ANY)),
        scratch_shapes=[
            VMEM((NZ, NH, rows, cols), BF16),
            VMEM((NX, NY, NC, depth, cols), BF16),
            VMEM(heads, BF16),
            VMEM(heads, BF16),
            pltpu.SemaphoreType.DMA((3,)),
            pltpu.SemaphoreType.DMA((40,)),
            pltpu.SemaphoreType.DMA((40,)),
        ],
        compiler_params=pltpu.CompilerParams(collective_id=0, has_side_effects=True),
    )(x, wq, k, v)


def attend_kernel(q_ref, kv_ref, wo_ref, o_ref, wog, ones_v, done, local_sem, send_sem, recv_sem):
    x, y, c, z, h = place()
    ys = [lax.rem(y + r, NY) for r in (1, 2, 3)]
    column = [blk_id(x, yp, c) for yp in ys]
    net = Links(send_sem, recv_sem)
    weights = Spread(net, wog, x, y, c)
    ready = greet([weights.right, weights.left, weights.other] + column)
    keys = kv_ref.shape[0]
    chunk = 1024
    factor = 1.0 / (math.sqrt(HEAD_DIM) * math.log(2.0))

    lane = lax.broadcasted_iota(jnp.int32, (chunk, 2 * HEAD_DIM), 1)

    @pl.loop(0, keys // chunk)
    def _(i):
        at = pl.ds(pl.multiple_of(i * chunk, chunk), chunk)
        v = kv_ref[at, :].astype(F32)
        ones_v[at, :] = jnp.where(lane < HEAD_DIM, 1.0, v).astype(BF16)

    def attend(tile):
        q = q_ref[tile]
        rows = q.shape[0]

        def body(i, state):
            top, total = state
            at = pl.ds(pl.multiple_of(i * chunk, chunk), chunk)
            s = lax.dot_general(
                q, kv_ref[at, :], (((1,), (1,)), ((), ())), preferred_element_type=F32
            )
            new_top = jnp.maximum(top, jnp.max(s, axis=1, keepdims=True))
            p = jnp.exp2((s - new_top) * factor)
            rescale = jnp.exp2((top - new_top) * factor)
            total = total * rescale + jnp.dot(
                p.astype(BF16), ones_v[at, :], preferred_element_type=F32
            )
            return new_top, total

        start = (jnp.full((rows, 1), -jnp.inf, F32), jnp.zeros((rows, 2 * HEAD_DIM), F32))
        _, total = lax.fori_loop(0, keys // chunk, body, start, unroll=2)
        context = total[:, HEAD_DIM:] / total[:, :HEAD_DIM]
        return jnp.concatenate([context, context], axis=1).astype(BF16)

    ready()
    own = pltpu.make_async_copy(wo_ref, wog.at[x, y, c], local_sem)
    own.start()
    w_col = [net.send(wo_ref, wog.at[x, y, c], to) for to in column]
    own.wait()
    swaps = []
    steps = [lambda: weights.first(w_col), weights.second, weights.third]
    for i, (yp, to) in enumerate(zip(ys, column)):
        done[i] = attend(yp)
        steps[i]()
        swaps.append(net.send(done.at[i], o_ref.at[y], to))
    o_ref[y] = attend(y)
    weights.finish()
    arrive(swaps)
    net.drain()


def attend(q, kv, wo):
    depth, cols = wo.shape
    vmem = pl.BlockSpec(memory_space=VMEM)
    return pl.pallas_call(
        attend_kernel,
        name="attend",
        out_shape=(
            jax.ShapeDtypeStruct(q.shape, BF16),
            jax.ShapeDtypeStruct((NX, NY, NC, depth, cols), BF16),
        ),
        in_specs=[vmem] * 3,
        out_specs=(vmem, pl.BlockSpec(memory_space=pl.ANY)),
        scratch_shapes=[
            VMEM(kv.shape, BF16),
            VMEM((3,) + q.shape[1:], BF16),
            pltpu.SemaphoreType.DMA,
            pltpu.SemaphoreType.DMA((14,)),
            pltpu.SemaphoreType.DMA((14,)),
        ],
        compiler_params=pltpu.CompilerParams(collective_id=1, has_side_effects=True),
    )(q, kv, wo)


CUTS = 2


def output_kernel(c_ref, w_ref, o_ref, p, half_r, half_l, in_r, in_l, out_r, out_l, total, far_out, far_in,
                  send_sem, recv_sem):
    x, y, c, z, h = place()
    up, down = fsdp_id(lax.rem(z + 1, NZ), h), fsdp_id(lax.rem(z + NZ - 1, NZ), h)
    far = fsdp_id(z, 1 - h)
    ready = greet([up, down, far])
    net = Links(send_sem, recv_sem)
    width = p.shape[-1]
    piece = 512
    context = jnp.concatenate([c_ref[j][:, :HEAD_DIM] for j in range(c_ref.shape[0])], axis=1)
    opposite = lax.rem(z + 4, NZ)
    rs, ls = [], []
    for k in range(CUTS):
        for i in range(width // piece):
            part = lax.dot_general(
                context, w_ref[pl.ds(k * width + i * piece, piece), :],
                (((1,), (1,)), ((), ())), preferred_element_type=F32,
            ).astype(BF16)
            p[k, :, :, :, pl.ds(i * piece, piece)] = part.reshape(p.shape[1:4] + (piece,))
        if k == 0:
            ready()
        rs.append(net.send(p.at[k, opposite, 0], half_r.at[k], up))
        ls.append(net.send(p.at[k, opposite, 1], half_l.at[k], down))
    for s in range(3):
        ahead, behind = lax.rem(z + 3 - s, NZ), lax.rem(z + NZ - 3 + s, NZ)
        for k in range(CUTS):
            arrive([rs[k]])
            if s == 0:
                out_r[k, 0, 0] = (p[k, ahead, 0].astype(F32) + half_r[k].astype(F32)).astype(BF16)
                out_r[k, 0, 1] = p[k, ahead, 1]
            else:
                out_r[k, s] = (p[k, ahead].astype(F32) + in_r[k, s - 1].astype(F32)).astype(BF16)
            rs[k] = net.send(out_r.at[k, s], in_r.at[k, s], up)
            arrive([ls[k]])
            if s == 0:
                out_l[k, 0, 0] = p[k, behind, 0]
                out_l[k, 0, 1] = (p[k, behind, 1].astype(F32) + half_l[k].astype(F32)).astype(BF16)
            else:
                out_l[k, s] = (p[k, behind].astype(F32) + in_l[k, s - 1].astype(F32)).astype(BF16)
            ls[k] = net.send(out_l.at[k, s], in_l.at[k, s], down)
    fars = []
    for k in range(CUTS):
        arrive([rs[k], ls[k]])
        total[k] = p[k, z].astype(F32) + in_r[k, 2].astype(F32) + in_l[k, 2].astype(F32)
        far_out[k] = total[k, 1 - h].astype(BF16)
        fars.append(net.send(far_out.at[k], far_in.at[k], far))
    for k in range(CUTS):
        arrive([fars[k]])
        o_ref[:, pl.ds(k * width, width)] = (total[k, h] + far_in[k].astype(F32)).astype(BF16)
    net.drain()


def project_and_reduce(context, wo):
    rows, out = context.shape[1], wo.shape[0]
    mine = rows // (NZ * NH)
    one = (CUTS, mine, out // CUTS)
    two = (CUTS, NH, mine, out // CUTS)
    chain = (CUTS, 3, NH, mine, out // CUTS)
    vmem = pl.BlockSpec(memory_space=VMEM)
    return pl.pallas_call(
        output_kernel,
        name="project_and_reduce",
        out_shape=jax.ShapeDtypeStruct((mine, out), BF16),
        in_specs=[vmem] * 2,
        out_specs=vmem,
        scratch_shapes=[
            VMEM((CUTS, NZ, NH, mine, out // CUTS), BF16),
            VMEM(one, BF16), VMEM(one, BF16),
            VMEM(chain, BF16), VMEM(chain, BF16), VMEM(chain, BF16), VMEM(chain, BF16),
            VMEM(two, F32), VMEM(one, BF16), VMEM(one, BF16),
            pltpu.SemaphoreType.DMA((9 * CUTS,)),
            pltpu.SemaphoreType.DMA((9 * CUTS,)),
        ],
        compiler_params=pltpu.CompilerParams(collective_id=2, has_side_effects=True),
    )(context, wo)


def shards(decoder_states, w_query, w_out_t, enc_keys, enc_values):
    cols = w_out_t.shape[1]
    q, kv = queries_and_pairs(decoder_states, w_query, enc_keys, enc_values)
    context, wo = attend(q, kv.reshape(-1, 2 * HEAD_DIM), w_out_t)
    return project_and_reduce(context, wo.reshape(-1, cols))


def solution(mesh):
    spec = P("blk", "fsdp")
    return jax.shard_map(
        shards, mesh=mesh, in_specs=(spec,) * 5,
        out_specs=P(("blk", "fsdp"), None), check_vma=False,
    )
```

time: 625 us -> 127 us (0.20)
  waiting for transfers between devices: 544 us -> 0 us
  Pallas kernels: 0 us -> 125 us
  matrix products: 38.5 us -> 0 us
  other arithmetic: 15.7 us -> 0 us
  between operations: 13.5 us -> 0.02 us
  local copies, waits for them, and re-layouts: 12.8 us -> 1.57 us
    all_gather x5 -> x0, waiting for transfers between devices: 305 us -> none  [the longest x1 110 us: shards(): lax.all_gather(decoder_states, 'fsdp', axis=1, tiled=True)]
    reduce_scatter x1 -> x0, waiting for transfers between devices: 235 us -> none  [shards(): lax.psum_scatter(lax.dot_general(context, out_full, (((1,), (1,)), ((), (...]
    pallas_call x0 -> x3, Pallas kernels: none -> 125 us  [the longest x1 58.8 us: queries_and_pairs(): pl.pallas_call(queries_kernel, name='queries_and_pairs', out_shape=(jax.S...]
    dot_general x4 -> x0, matrix products: 38.5 us -> none  [the longest x1 15.5 us: absorb(): jnp.einsum('hqk,khd->hqd', probability.astype(jnp.bfloat16), value_heads,...]
    reduce_sum x1 -> x0, other arithmetic: 14.1 us -> none  [absorb(): running_sum = running_sum * rescale + jnp.sum(probability, axis=2)]
    all_gather x2 -> x0, local copies, waits for them, and re-layouts: 12.8 us -> none  [the longest x1 6.4 us: shards(): lax.all_gather(enc_values, 'blk', axis=0, tiled=True)]
  transfers between devices with their start and end apart: 6 -> 0, of which waited for: 6 -> 0; matrix products, arithmetic and copies ran while one was open for 10% -> 0% of each run, Pallas kernels for 0% -> 0%
where the time goes in v2:
time: 127 us; the launch traced here: 126 us
  Pallas kernels  125 us (98%)
  local copies, waits for them, and re-layouts  1.57 us (1%)
    pallas_call x1, Pallas kernels, queries_and_pairs(): pl.pallas_call(queries_kernel, name='queries_and_pairs', out_shape=(jax.S...  58.8 us
    pallas_call x1, Pallas kernels, project_and_reduce(): pl.pallas_call(output_kernel, name='project_and_reduce', out_shape=jax.Sh...  36.6 us
    pallas_call x1, Pallas kernels, attend(): pl.pallas_call(attend_kernel, name='attend', out_shape=(jax.ShapeDtypeStr...  29.4 us

profile of v2, /device:TPU:8, one launch (start us, length us, event | category | flops | bytes accessed | tf_op | source)
XLA Modules:
  0.0 126.4 jit_solution(6075206824321087593)
XLA Ops:
  0.0 58.8 %queries_and_pairs.1 = (bf16[4,256,128]{2,1,0:T(8,128)(2,1)}, bf16[4,4,2,256,128]{4,3,2,1,0:T(8,128)(2,1)}) custom-call(bf16[256,256]{1,0:T(8,128)(2,1)} %x_ref.1, bf16[128,256]{1,0:T(8,128)(2,1)} %wq_ref.1, bf16[256,256]{1,0:T(8,128)(2,1)} %k_ref.1, bf16[256,256]{1,0:T(8,128)(2,1)} %v_ref.1), custom_call_target="tpu_custom_call" | custom-call | tf_op jit(solution)/shard_map/queries_and_pairs/pallas_call | solution.py:184
  58.8 29.4 %attend.1 = (bf16[4,256,128]{2,1,0:T(8,128)(2,1)}, bf16[4,4,2,128,256]{4,3,2,1,0:T(8,128)(2,1)}) custom-call(bf16[4,256,128]{2,1,0:T(8,128)(2,1)} %get-tuple-element.9.q_ref, bf16[8192,128]{1,0:T(8,128)(2,1)} %bitcast.2, bf16[128,256]{1,0:T(8,128)(2,1)} %wo_ref.1), custom_call_target="tpu_custom_call" | custom-call | tf_op jit(solution)/shard_map/attend/pallas_call | solution.py:268
  88.2 36.6 %project_and_reduce.1 = bf16[16,4096]{1,0:T(8,128)(2,1)} custom-call(bf16[4,256,128]{2,1,0:T(8,128)(2,1)} %get-tuple-element.11.c_ref, bf16[4096,256]{1,0:T(8,128)(2,1)} %bitcast.3), custom_call_target="tpu_custom_call" | custom-call | tf_op jit(solution)/shard_map/project_and_reduce/pallas_call | solution.py:350
  124.8 1.6 %copy.7 = bf16[16,4096]{1,0:T(8,128)(2,1)} copy(bf16[16,4096]{1,0:T(8,128)(2,1)} %project_and_reduce.1) | data formatting | bytes 262144

commit v3 on v2

--- a/solution.py
+++ b/solution.py
@@ -66,30 +66,47 @@
     def __init__(self, net, buf, x, y, c):
         self.net, self.buf, self.c, self.x = net, buf, c, x
         self.xs = [lax.rem(x + r, NX) for r in (1, 2, 3)]
+        self.ys = [lax.rem(y + r, NY) for r in range(NY)]
         self.right, self.left = blk_id(self.xs[0], y, c), blk_id(self.xs[2], y, c)
         self.other = blk_id(x, y, 1 - c)
-        self.cores = []
+        self.column = [blk_id(x, yp, c) for yp in self.ys]
+        self.hops, self.halves, self.cores = [None] * NY, [None] * NY, []
+
+    def spread_y(self, pieces):
+        at = self.buf.at[self.x, self.ys[0], self.c]
+        self.got = [
+            self.net.send(piece, at, to) for piece, to in zip(pieces[1:], self.column[1:])
+        ]
+
+    def first(self, r, piece=None):
+        at = self.buf.at[self.x, self.ys[r], self.c]
+        if r > 0:
+            arrive([self.got[NY - 1 - r]])
+        src = at if piece is None else piece
+        self.hops[r] = (self.net.send(src, at, self.right), self.net.send(src, at, self.left))
+
+    def second(self, r):
+        arrive(self.hops[r])
+        if r < 2:
+            at = self.buf.at[self.xs[2], self.ys[r], self.c]
+            self.halves[r] = self.net.send(at, at, self.right)
+        else:
+            at = self.buf.at[self.xs[0], self.ys[r], self.c]
+            self.halves[r] = self.net.send(at, at, self.left)
 
     def to_core(self, *xs):
         for at in xs:
             block = self.buf.at[at, :, self.c]
             self.cores.append(self.net.send(block, block, self.other))
 
-    def first(self, arrivals):
-        arrive(arrivals)
-        block = self.buf.at[self.x, :, self.c]
-        self.hop = (self.net.send(block, block, self.right), self.net.send(block, block, self.left))
+    def core_own(self):
         self.to_core(self.x)
 
-    def second(self):
-        arrive(self.hop)
-        a = self.buf.at[self.xs[2], pl.ds(0, 2), self.c]
-        b = self.buf.at[self.xs[0], pl.ds(2, 2), self.c]
-        self.hop = (self.net.send(a, a, self.right), self.net.send(b, b, self.left))
+    def core_near(self):
         self.to_core(self.xs[0], self.xs[2])
 
-    def third(self):
-        arrive(self.hop)
+    def core_far(self):
+        arrive(self.halves)
         self.to_core(self.xs[1])
 
     def finish(self):
@@ -109,20 +126,43 @@
         cols = slice(j * HEAD_DIM, (j + 1) * HEAD_DIM)
         kv[j] = jnp.concatenate([k_ref[:, cols], v_ref[:, cols]], axis=1)
     ready()
-
-    def ring(s, part, is_own, both):
-        a, b = lax.rem(z + NZ - s, NZ), lax.rem(z + s, NZ)
+    steps = []
+
+    def at_time(when, step, *args):
+        steps.append((when, len(steps), lambda: step(*args)))
+
+    def ring(key, s, part, first_row, count, is_own, ways):
+        if s > 0:
+            arrive(rings[key])
+        row = pl.ds(first_row, count)
         sent = []
-        if both != "down":
-            src = x_ref if is_own and s == 0 else xg.at[a, part]
-            sent.append(net.send(src, xg.at[a, part], up))
-        if both != "up":
-            src = x_ref if is_own and s == 0 else xg.at[b, part]
-            sent.append(net.send(src, xg.at[b, part], down))
-        return sent
-
-    pair = net.send(x_ref, xg.at[z, h], far)
-    own_ring = ring(0, h, True, "both")
+        for way, to, slot in (("up", up, lax.rem(z + NZ - s, NZ)), ("down", down, lax.rem(z + s, NZ))):
+            if way in ways:
+                at = xg.at[slot, part, row]
+                sent.append(net.send(x_ref.at[row] if is_own and s == 0 else at, at, to))
+        rings[key] = sent
+
+    rings = {}
+    both = ("up", "down")
+    rows = x_ref.shape[0]
+    for j in range(2):
+        for s in range(4):
+            at_time(4 * s + j, ring, ("own", j), s, h, j * (rows // 2), rows // 2, True, both if s < 3 else ("up",))
+    pair = []
+    quarter = rows // 4
+    for j in range(4):
+        row = pl.ds(j * quarter, quarter)
+        pair.append(net.send(x_ref.at[row], xg.at[z, h, row], far))
+
+        def start(j=j):
+            arrive([pair[j]])
+            ring(("far", j), 0, 1 - h, j * quarter, quarter, False, both)
+
+        base = 6.5 + 1.7 * j
+        at_time(base, start)
+        for s in range(1, 4):
+            at_time(base + 3.8 * s, ring, ("far", j), s, 1 - h, j * quarter, quarter, False,
+                    both if s < 3 else ("down",))
     own = [
         pltpu.make_async_copy(x_ref, xg.at[z, h], local_sem.at[0]),
         pltpu.make_async_copy(wq_ref, wqg.at[x, y, c], local_sem.at[1]),
@@ -130,33 +170,30 @@
     ]
     for copy in own:
         copy.start()
-    w_col = [net.send(wq_ref, wqg.at[x, y, c], to) for to in column]
-    kv_col = [net.send(kv.at[yp], kvg.at[x, y, c], to) for yp, to in zip(ys, column)]
-    for copy in own:
-        copy.wait()
-    arrive(own_ring)
-    own_ring = ring(1, h, True, "both")
-    weights.first(w_col)
-    arrive(own_ring)
-    own_ring = ring(2, h, True, "both")
-    arrive([pair])
-    far_ring = ring(0, 1 - h, False, "both")
-    pairs.first(kv_col)
-    arrive(own_ring)
-    own_ring = ring(3, h, True, "up")
-    weights.second()
-    arrive(far_ring)
-    far_ring = ring(1, 1 - h, False, "both")
-    weights.third()
-    pairs.second()
-    arrive(far_ring)
-    far_ring = ring(2, 1 - h, False, "both")
-    pairs.third()
-    arrive(own_ring)
-    arrive(far_ring)
-    far_ring = ring(3, 1 - h, False, "down")
+
+    def own_done():
+        for copy in own:
+            copy.wait()
+
+    at_time(3.2, own_done)
+    at_time(0.1, weights.spread_y, [wq_ref] * NY)
+    at_time(0.2, weights.first, 0, wq_ref)
+    at_time(3.5, pairs.spread_y, [kv.at[yp] for yp in pairs.ys])
+    at_time(3.6, pairs.first, 0, kv.at[y])
+    for unit, base in ((weights, 6.0), (pairs, 14.0)):
+        for k, r in enumerate((3, 2, 1)):
+            at_time(base + 1.7 * k, unit.first, r)
+        at_time(base + 0.5, unit.second, 0)
+        for k, r in enumerate((3, 2, 1)):
+            at_time(base + 6 + 1.7 * k, unit.second, r)
+        at_time(base + 3.6, unit.core_own)
+        at_time(base + 9.6, unit.core_near)
+        at_time(base + 13, unit.core_far)
+    for _, _, step in sorted(steps, key=lambda item: item[:2]):
+        step()
+    for sent in rings.values():
+        arrive(sent)
     weights.finish()
-    arrive(far_ring)
 
     total = None
     for f in range(NZ * NH):
@@ -196,8 +233,8 @@
             VMEM(heads, BF16),
             VMEM(heads, BF16),
             pltpu.SemaphoreType.DMA((3,)),
-            pltpu.SemaphoreType.DMA((40,)),
-            pltpu.SemaphoreType.DMA((40,)),
+            pltpu.SemaphoreType.DMA((88,)),
+            pltpu.SemaphoreType.DMA((88,)),
         ],
         compiler_params=pltpu.CompilerParams(collective_id=0, has_side_effects=True),
     )(x, wq, k, v)
@@ -241,17 +278,30 @@
             return new_top, total
 
         start = (jnp.full((rows, 1), -jnp.inf, F32), jnp.zeros((rows, 2 * HEAD_DIM), F32))
-        _, total = lax.fori_loop(0, keys // chunk, body, start, unroll=2)
+        _, total = lax.fori_loop(0, keys // chunk, body, start, unroll=4)
         context = total[:, HEAD_DIM:] / total[:, :HEAD_DIM]
         return jnp.concatenate([context, context], axis=1).astype(BF16)
 
     ready()
     own = pltpu.make_async_copy(wo_ref, wog.at[x, y, c], local_sem)
     own.start()
-    w_col = [net.send(wo_ref, wog.at[x, y, c], to) for to in column]
+    weights.spread_y([wo_ref] * NY)
+    weights.first(0, wo_ref)
     own.wait()
     swaps = []
-    steps = [lambda: weights.first(w_col), weights.second, weights.third]
+
+    def near():
+        for r in (3, 2, 1):
+            weights.first(r)
+        weights.core_own()
+        weights.second(0)
+
+    def across():
+        for r in (3, 2, 1):
+            weights.second(r)
+        weights.core_near()
+
+    steps = [near, across, weights.core_far]
     for i, (yp, to) in enumerate(zip(ys, column)):
         done[i] = attend(yp)
         steps[i]()
@@ -278,14 +328,14 @@
             VMEM(kv.shape, BF16),
             VMEM((3,) + q.shape[1:], BF16),
             pltpu.SemaphoreType.DMA,
-            pltpu.SemaphoreType.DMA((14,)),
-            pltpu.SemaphoreType.DMA((14,)),
+            pltpu.SemaphoreType.DMA((22,)),
+            pltpu.SemaphoreType.DMA((22,)),
         ],
         compiler_params=pltpu.CompilerParams(collective_id=1, has_side_effects=True),
     )(q, kv, wo)
 
 
-CUTS = 2
+CUTS = 4
 
 
 def output_kernel(c_ref, w_ref, o_ref, p, half_r, half_l, in_r, in_l, out_r, out_l, total, far_out, far_in,

time: 127 us -> 118 us (0.929)
  Pallas kernels: 125 us -> 116 us
    pallas_call x1, Pallas kernels: 29.4 us -> 24.6 us  [attend(): pl.pallas_call(attend_kernel, name='attend', out_shape=(jax.ShapeDtypeStr...]
    pallas_call x1, Pallas kernels: 36.6 us -> 33.9 us  [project_and_reduce(): pl.pallas_call(output_kernel, name='project_and_reduce', out_shape=jax.Sh...]
where the time goes in v3:
time: 118 us
  Pallas kernels  116 us (98%)
  local copies, waits for them, and re-layouts  1.57 us (1%)
    pallas_call x1, Pallas kernels, queries_and_pairs(): pl.pallas_call(queries_kernel, name='queries_and_pairs', out_shape=(jax.S...  57.7 us
    pallas_call x1, Pallas kernels, project_and_reduce(): pl.pallas_call(output_kernel, name='project_and_reduce', out_shape=jax.Sh...  33.9 us
    pallas_call x1, Pallas kernels, attend(): pl.pallas_call(attend_kernel, name='attend', out_shape=(jax.ShapeDtypeStr...  24.6 us

profile of v3, /device:TPU:8, one launch (start us, length us, event | category | flops | bytes accessed | tf_op | source)
XLA Modules:
  0.0 117.8 jit_solution(5122488754725041319)
XLA Ops:
  0.0 57.7 %queries_and_pairs.1 = (bf16[4,256,128]{2,1,0:T(8,128)(2,1)}, bf16[4,4,2,256,128]{4,3,2,1,0:T(8,128)(2,1)}) custom-call(bf16[256,256]{1,0:T(8,128)(2,1)} %x_ref.1, bf16[128,256]{1,0:T(8,128)(2,1)} %wq_ref.1, bf16[256,256]{1,0:T(8,128)(2,1)} %k_ref.1, bf16[256,256]{1,0:T(8,128)(2,1)} %v_ref.1), custom_call_target="tpu_custom_call" | custom-call | tf_op jit(solution)/shard_map/queries_and_pairs/pallas_call | solution.py:221
  57.7 24.6 %attend.1 = (bf16[4,256,128]{2,1,0:T(8,128)(2,1)}, bf16[4,4,2,128,256]{4,3,2,1,0:T(8,128)(2,1)}) custom-call(bf16[4,256,128]{2,1,0:T(8,128)(2,1)} %get-tuple-element.9.q_ref, bf16[8192,128]{1,0:T(8,128)(2,1)} %bitcast.2, bf16[128,256]{1,0:T(8,128)(2,1)} %wo_ref.1), custom_call_target="tpu_custom_call" | custom-call | tf_op jit(solution)/shard_map/attend/pallas_call | solution.py:318
  82.4 33.9 %project_and_reduce.1 = bf16[16,4096]{1,0:T(8,128)(2,1)} custom-call(bf16[4,256,128]{2,1,0:T(8,128)(2,1)} %get-tuple-element.11.c_ref, bf16[4096,256]{1,0:T(8,128)(2,1)} %bitcast.3), custom_call_target="tpu_custom_call" | custom-call | tf_op jit(solution)/shard_map/project_and_reduce/pallas_call | solution.py:400
  116.2 1.6 %copy.7 = bf16[16,4096]{1,0:T(8,128)(2,1)} copy(bf16[16,4096]{1,0:T(8,128)(2,1)} %project_and_reduce.1) | data formatting | bytes 262144

commit v4 on v3

--- a/solution.py
+++ b/solution.py
@@ -176,11 +176,11 @@
             copy.wait()
 
     at_time(3.2, own_done)
-    at_time(0.1, weights.spread_y, [wq_ref] * NY)
+    at_time(4.2, weights.spread_y, [wq_ref] * NY)
     at_time(0.2, weights.first, 0, wq_ref)
-    at_time(3.5, pairs.spread_y, [kv.at[yp] for yp in pairs.ys])
+    at_time(11.5, pairs.spread_y, [kv.at[yp] for yp in pairs.ys])
     at_time(3.6, pairs.first, 0, kv.at[y])
-    for unit, base in ((weights, 6.0), (pairs, 14.0)):
+    for unit, base in ((weights, 10.5), (pairs, 19.0)):
         for k, r in enumerate((3, 2, 1)):
             at_time(base + 1.7 * k, unit.first, r)
         at_time(base + 0.5, unit.second, 0)
@@ -203,9 +203,9 @@
         )
         total = part if total is None else total + part
     q = total.astype(BF16)
-    zero = jnp.zeros((q.shape[0], HEAD_DIM), BF16)
     for j in range(NY):
-        qs[j] = jnp.concatenate([q[:, j * HEAD_DIM:(j + 1) * HEAD_DIM], zero], axis=1)
+        head = q[:, j * HEAD_DIM:(j + 1) * HEAD_DIM]
+        qs[j] = jnp.concatenate([head[:rows // 2], head[rows // 2:]], axis=1)
     swaps = [net.send(qs.at[yp], q_ref.at[y], to) for yp, to in zip(ys, column)]
     q_ref[y] = qs[y]
     pairs.finish()
@@ -217,12 +217,13 @@
     rows, cols = x.shape
     depth = wq.shape[0]
     heads = (NY, rows, 2 * HEAD_DIM)
+    packed = (NY, rows // 2, 2 * HEAD_DIM)
     vmem = pl.BlockSpec(memory_space=VMEM)
     return pl.pallas_call(
         queries_kernel,
         name="queries_and_pairs",
         out_shape=(
-            jax.ShapeDtypeStruct(heads, BF16),
+            jax.ShapeDtypeStruct(packed, BF16),
             jax.ShapeDtypeStruct((NX, NY, NC, rows, 2 * HEAD_DIM), BF16),
         ),
         in_specs=[vmem] * 4,
@@ -231,7 +232,7 @@
             VMEM((NZ, NH, rows, cols), BF16),
             VMEM((NX, NY, NC, depth, cols), BF16),
             VMEM(heads, BF16),
-            VMEM(heads, BF16),
+            VMEM(packed, BF16),
             pltpu.SemaphoreType.DMA((3,)),
             pltpu.SemaphoreType.DMA((88,)),
             pltpu.SemaphoreType.DMA((88,)),
@@ -248,7 +249,7 @@
     weights = Spread(net, wog, x, y, c)
     ready = greet([weights.right, weights.left, weights.other] + column)
     keys = kv_ref.shape[0]
-    chunk = 1024
+    chunk = 2048
     factor = 1.0 / (math.sqrt(HEAD_DIM) * math.log(2.0))
 
     lane = lax.broadcasted_iota(jnp.int32, (chunk, 2 * HEAD_DIM), 1)
@@ -260,7 +261,12 @@
         ones_v[at, :] = jnp.where(lane < HEAD_DIM, 1.0, v).astype(BF16)
 
     def attend(tile):
-        q = q_ref[tile]
+        two = q_ref[tile]
+        zero = jnp.zeros((two.shape[0], HEAD_DIM), BF16)
+        q = jnp.concatenate([
+            jnp.concatenate([two[:, :HEAD_DIM], zero], axis=1),
+            jnp.concatenate([two[:, HEAD_DIM:], zero], axis=1),
+        ], axis=0)
         rows = q.shape[0]
 
         def body(i, state):
@@ -314,19 +320,20 @@
 
 def attend(q, kv, wo):
     depth, cols = wo.shape
+    context = (q.shape[0], 2 * q.shape[1], q.shape[2])
     vmem = pl.BlockSpec(memory_space=VMEM)
     return pl.pallas_call(
         attend_kernel,
         name="attend",
         out_shape=(
-            jax.ShapeDtypeStruct(q.shape, BF16),
+            jax.ShapeDtypeStruct(context, BF16),
             jax.ShapeDtypeStruct((NX, NY, NC, depth, cols), BF16),
         ),
         in_specs=[vmem] * 3,
         out_specs=(vmem, pl.BlockSpec(memory_space=pl.ANY)),
         scratch_shapes=[
             VMEM(kv.shape, BF16),
-            VMEM((3,) + q.shape[1:], BF16),
+            VMEM((3,) + context[1:], BF16),
             pltpu.SemaphoreType.DMA,
             pltpu.SemaphoreType.DMA((22,)),
             pltpu.SemaphoreType.DMA((22,)),

time: 118 us -> 115 us (0.975)
  the two profiles are of different devices: /device:TPU:8 before, /device:TPU:16 now
where the time goes in v4:
time: 115 us; the launch traced here: 114 us
  Pallas kernels  113 us (98%)
  local copies, waits for them, and re-layouts  1.57 us (1%)
    pallas_call x1, Pallas kernels, queries_and_pairs(): pl.pallas_call(queries_kernel, name='queries_and_pairs', out_shape=(jax.S...  53.7 us
    pallas_call x1, Pallas kernels, project_and_reduce(): pl.pallas_call(output_kernel, name='project_and_reduce', out_shape=jax.Sh...  33.7 us
    pallas_call x1, Pallas kernels, attend(): pl.pallas_call(attend_kernel, name='attend', out_shape=(jax.ShapeDtypeStr...  25.4 us

profile of v4, /device:TPU:16, one launch (start us, length us, event | category | flops | bytes accessed | tf_op | source)
XLA Modules:
  0.0 114.4 jit_solution(9130959891759273217)
XLA Ops:
  0.0 53.7 %queries_and_pairs.1 = (bf16[4,128,128]{2,1,0:T(8,128)(2,1)}, bf16[4,4,2,256,128]{4,3,2,1,0:T(8,128)(2,1)}) custom-call(bf16[256,256]{1,0:T(8,128)(2,1)} %x_ref.1, bf16[128,256]{1,0:T(8,128)(2,1)} %wq_ref.1, bf16[256,256]{1,0:T(8,128)(2,1)} %k_ref.1, bf16[256,256]{1,0:T(8,128)(2,1)} %v_ref.1), custom_call_target="tpu_custom_call" | custom-call | tf_op jit(solution)/shard_map/queries_and_pairs/pallas_call | solution.py:222
  53.7 25.4 %attend.1 = (bf16[4,256,128]{2,1,0:T(8,128)(2,1)}, bf16[4,4,2,128,256]{4,3,2,1,0:T(8,128)(2,1)}) custom-call(bf16[4,128,128]{2,1,0:T(8,128)(2,1)} %get-tuple-element.9.q_ref, bf16[8192,128]{1,0:T(8,128)(2,1)} %bitcast.3, bf16[128,256]{1,0:T(8,128)(2,1)} %wo_ref.1), custom_call_target="tpu_custom_call" | custom-call | tf_op jit(solution)/shard_map/attend/pallas_call | solution.py:325
  79.1 33.7 %project_and_reduce.1 = bf16[16,4096]{1,0:T(8,128)(2,1)} custom-call(bf16[4,256,128]{2,1,0:T(8,128)(2,1)} %get-tuple-element.11.c_ref, bf16[4096,256]{1,0:T(8,128)(2,1)} %bitcast.2), custom_call_target="tpu_custom_call" | custom-call | tf_op jit(solution)/shard_map/project_and_reduce/pallas_call | solution.py:407
  112.8 1.6 %copy.7 = bf16[16,4096]{1,0:T(8,128)(2,1)} copy(bf16[16,4096]{1,0:T(8,128)(2,1)} %project_and_reduce.1) | data formatting | bytes 262144

commit v5 on v4

--- a/solution.py
+++ b/solution.py
@@ -176,11 +176,11 @@
             copy.wait()
 
     at_time(3.2, own_done)
-    at_time(4.2, weights.spread_y, [wq_ref] * NY)
+    at_time(5.5, weights.spread_y, [wq_ref] * NY)
     at_time(0.2, weights.first, 0, wq_ref)
-    at_time(11.5, pairs.spread_y, [kv.at[yp] for yp in pairs.ys])
+    at_time(6.8, pairs.spread_y, [kv.at[yp] for yp in pairs.ys])
     at_time(3.6, pairs.first, 0, kv.at[y])
-    for unit, base in ((weights, 10.5), (pairs, 19.0)):
+    for unit, base in ((weights, 11.5), (pairs, 15.0)):
         for k, r in enumerate((3, 2, 1)):
             at_time(base + 1.7 * k, unit.first, r)
         at_time(base + 0.5, unit.second, 0)

time: 115 us -> 112 us (0.974)
  Pallas kernels: 113 us -> 110 us
    pallas_call x1, Pallas kernels: 53.7 us -> 52.2 us  [queries_and_pairs(): pl.pallas_call(queries_kernel, name='queries_and_pairs', out_shape=(jax.S...]
    pallas_call x1, Pallas kernels: 33.7 us -> 32.5 us  [project_and_reduce(): pl.pallas_call(output_kernel, name='project_and_reduce', out_shape=jax.Sh...]
where the time goes in v5:
time: 112 us
  Pallas kernels  110 us (98%)
  local copies, waits for them, and re-layouts  1.57 us (1%)
    pallas_call x1, Pallas kernels, queries_and_pairs(): pl.pallas_call(queries_kernel, name='queries_and_pairs', out_shape=(jax.S...  52.2 us
    pallas_call x1, Pallas kernels, project_and_reduce(): pl.pallas_call(output_kernel, name='project_and_reduce', out_shape=jax.Sh...  32.5 us
    pallas_call x1, Pallas kernels, attend(): pl.pallas_call(attend_kernel, name='attend', out_shape=(jax.ShapeDtypeStr...  25.6 us

profile of v5, /device:TPU:16, one launch (start us, length us, event | category | flops | bytes accessed | tf_op | source)
XLA Modules:
  0.0 111.8 jit_solution(10196964914641506015)
XLA Ops:
  0.0 52.2 %queries_and_pairs.1 = (bf16[4,128,128]{2,1,0:T(8,128)(2,1)}, bf16[4,4,2,256,128]{4,3,2,1,0:T(8,128)(2,1)}) custom-call(bf16[256,256]{1,0:T(8,128)(2,1)} %x_ref.1, bf16[128,256]{1,0:T(8,128)(2,1)} %wq_ref.1, bf16[256,256]{1,0:T(8,128)(2,1)} %k_ref.1, bf16[256,256]{1,0:T(8,128)(2,1)} %v_ref.1), custom_call_target="tpu_custom_call" | custom-call | tf_op jit(solution)/shard_map/queries_and_pairs/pallas_call | solution.py:222
  52.2 25.6 %attend.1 = (bf16[4,256,128]{2,1,0:T(8,128)(2,1)}, bf16[4,4,2,128,256]{4,3,2,1,0:T(8,128)(2,1)}) custom-call(bf16[4,128,128]{2,1,0:T(8,128)(2,1)} %get-tuple-element.9.q_ref, bf16[8192,128]{1,0:T(8,128)(2,1)} %bitcast.3, bf16[128,256]{1,0:T(8,128)(2,1)} %wo_ref.1), custom_call_target="tpu_custom_call" | custom-call | tf_op jit(solution)/shard_map/attend/pallas_call | solution.py:325
  77.8 32.5 %project_and_reduce.1 = bf16[16,4096]{1,0:T(8,128)(2,1)} custom-call(bf16[4,256,128]{2,1,0:T(8,128)(2,1)} %get-tuple-element.11.c_ref, bf16[4096,256]{1,0:T(8,128)(2,1)} %bitcast.2), custom_call_target="tpu_custom_call" | custom-call | tf_op jit(solution)/shard_map/project_and_reduce/pallas_call | solution.py:407
  110.2 1.6 %copy.7 = bf16[16,4096]{1,0:T(8,128)(2,1)} copy(bf16[16,4096]{1,0:T(8,128)(2,1)} %project_and_reduce.1) | data formatting | bytes 262144
